TPU v7x, 32 devices: a whole 2x2x4 slice. The times are simulated.
32 devices in a mesh: grp: 2 (over x), chan: 16 (over z, y, core).
Axes of the slice: x: 2, y: 2, z: 4, core: 2. Of those that a mesh axis runs over, the one named last changes fastest.
Arguments:
- spectra: bfloat16 [2048, 2, 64, 512], P(('grp', 'chan')), parts along dimension 0, may hold values from -6 to 6
- valid: int32 [2048, 64], P(('grp', 'chan')), parts along dimension 0, may hold values 0 or 1
- sources: int32 [32], P('grp'), parts along dimension 0, may hold values from 0 to 1023
Outputs:
- smoothed: float32 [32, 1024, 1024], P('grp', 'chan'), parts along dimension 0
There are 2 independent parts, one for each index of `grp`. A program takes and returns all parts, laid end to end along the dimension named above; each array names one. Nothing has to cross between parts.
Inputs may be any that keep to these rules, and one draw needn't show every extreme that they name: `sources`: channel indices of the segment; repeats may occur.
All inputs are finite; a program needn't handle non-finite values. No bound on the sum of `valid` on one device may be relied on, other than what follows from the above.
Results may differ from a plain program's by a relative error of at most 0.0037.
Values may be sent and summed in bfloat16 or wider, within the bound.
A program may use at most 128 MiB of HBM per device.

v0:
```python
import jax
import jax.numpy as jnp
from jax import lax
from jax.sharding import PartitionSpec as P


def with_halo(array, sides, width):
    for axis, dim in sides:
        size, length = (lax.axis_size(axis), array.shape[dim])
        up = [(i, (i + 1) % size) for i in range(size - 1)]
        down = [(j, i) for i, j in up]
        last = lax.slice_in_dim(array, length - width, length, axis=dim)
        leading = lax.slice_in_dim(array, 0, width, axis=dim)
        before = lax.ppermute(last, axis, up)
        after = lax.ppermute(leading, axis, down)
        array = jnp.concatenate([before, array, after], axis=dim)
    return array


def make_table(nbins, nlags):
    freq = jnp.arange(nbins, dtype=jnp.int32)
    lagidx = jnp.arange(nlags, dtype=jnp.int32)
    phase = (freq[:, None] * lagidx[None, :] % nlags).astype(jnp.float32)
    angle = 2.0 * jnp.pi * phase / nlags
    weight = jnp.where(freq == 0, 1.0, 2.0).astype(jnp.float32) / nlags
    cosine = weight[:, None] * jnp.cos(angle)
    sine = -weight[:, None] * jnp.sin(angle)
    return jnp.concatenate([cosine, sine], axis=0).astype(jnp.bfloat16)


def contract(left, right):
    return lax.dot_general(
        left, right, (((1,), (1,)), ((2,), (2,))), preferred_element_type=jnp.float32
    )


def to_lags(cross, table):
    nsrc, nrow, width = cross.shape
    flat = cross.reshape(nsrc * nrow, width)
    return jnp.dot(flat, table, preferred_element_type=jnp.float32).reshape(
        nsrc, nrow, table.shape[1]
    )


def local(spectra, valid, sources):
    nchan, _, nwin, nbins = spectra.shape
    nsrc = sources.shape[0]
    nlags = 2 * nbins
    me_idx = lax.axis_index("chan")
    owner = sources // nchan
    local_idx = sources - me_idx * nchan
    chan_valid = valid.astype(jnp.float32)
    columns = jnp.arange(nchan, dtype=jnp.int32)
    picker = ((local_idx[:, None] == columns[None, :]) & (owner == me_idx)[:, None]).astype(
        jnp.bfloat16
    )
    picked = jnp.dot(
        picker, spectra.reshape(nchan, 2 * nwin * nbins), preferred_element_type=jnp.float32
    )
    picked_valid = jnp.dot(picker.astype(jnp.float32), chan_valid)
    got, got_valid = lax.psum((picked, picked_valid), "chan")
    src_spec = got.astype(jnp.bfloat16).reshape(nsrc, 2, nwin, nbins)
    src_m = src_spec * got_valid.astype(jnp.bfloat16)[:, None, :, None]
    chan_m = spectra * chan_valid.astype(jnp.bfloat16)[:, None, :, None]
    real_part = (contract(src_m[:, 0], chan_m[:, 0]) + contract(src_m[:, 1], chan_m[:, 1])) / nwin
    imag_part = (contract(src_m[:, 0], chan_m[:, 1]) - contract(src_m[:, 1], chan_m[:, 0])) / nwin
    stacked = jnp.concatenate([real_part, imag_part], axis=0)
    cross = jnp.transpose(stacked, (1, 2, 0)).astype(jnp.bfloat16)
    table = make_table(nbins, nlags)
    lags = to_lags(cross, table)
    extended = with_halo(lags, (("chan", 1),), 2)
    total = extended[:, 0:nchan] + extended[:, 1 : nchan + 1] + extended[:, 2 : nchan + 2]
    total = total + extended[:, 3 : nchan + 3] + extended[:, 4 : nchan + 4]
    return total / 5.0


def solution(mesh):
    in_specs = (P(("grp", "chan"), None, None, None), P(("grp", "chan"), None), P("grp"))
    out_specs = P("grp", "chan", None)
    return jax.shard_map(local, mesh=mesh, in_specs=in_specs, out_specs=out_specs, check_vma=False)
```

profile of v0, /device:TPU:0, one launch (start us, length us, event | category | flops | bytes accessed | tf_op | source)
XLA Modules:
  0.0 235.0 jit_solution(4453375088177944246)
XLA Ops:
  0.0 0.7 fusion.29
  0.7 0.7 broadcast_subtract_fusion
  1.3 0.0 copy-start.2
  1.3 11.8 %copy.12 = bf16[8,8,128,512]{3,1,2,0:T(8,128)(2,1)} copy(bf16[8,8,128,512]{3,2,1,0:T(8,128)(2,1)} %bitcast.31) | data formatting | bytes 16777216
  13.1 0.0 copy-done.2
  13.1 0.2 fusion.18
  13.3 6.7 %fusion.22 = f32[16,65536]{1,0:T(8,128)} fusion(bf16[64,65536]{1,0:T(8,128)(2,1)} %bitcast.32, s32[16]{0:T(128)S(1)} %broadcast_subtract_fusion, pred[16]{0:T(512)(128)(4,1)S(1)} %fusion.29), kind=kOutput, calls=%fused_computation.44 | convolution fusion | flops 134219776 | bytes 12582992 | tf_op jit(solution)/shard_map/dot_general | solution.py:57
  19.9 102.5 %all-reduce.2 = (bf16[16,65536]{1,0:T(8,128)(2,1)S(1)}, bf16[16,64]{1,0:T(8,128)(2,1)S(1)}) all-reduce(f32[16,65536]{1,0:T(8,128)} %fusion.22, f32[16,64]{1,0:T(8,128)S(1)} %fusion.18), channel_id=1, replica_groups=mesh['grp'=2,'chan'=16] {'chan'}, use_global_device_ids=true, to_apply=%region_0.1 | all-reduce | flops 1049600 | bytes 6297600 | tf_op jit(solution)/shard_map/psum | solution.py:61
  122.4 0.7 copy.13
  123.1 0.2 broadcast_multiply_fusion.1
  123.3 1.1 slice_bitcast_fusion.2
  124.4 3.0 %copy.4 = bf16[16,64,512]{1,0,2:T(8,128)(2,1)S(1)} copy(bf16[16,64,512]{2,1,0:T(8,128)(2,1)} %get-tuple-element.12) | data formatting | bytes 2097152 | tf_op jit(solution)/shard_map/squeeze | solution.py:65
  127.4 7.2 %broadcast_multiply_fusion = bf16[64,2,64,512]{3,2,1,0:T(8,128)(2,1)} fusion(bf16[64,2,64,512]{3,2,1,0:T(8,128)(2,1)} %param.3, bf16[64,64]{1,0:T(8,128)(2,1)S(1)} %convert_convert_fusion), kind=kLoop, calls=%fused_computation.15 | loop fusion | flops 4194304 | bytes 16785408 | tf_op jit(solution)/shard_map/mul | solution.py:64
  134.6 6.1 %slice_bitcast_fusion.1 = (bf16[64,64,512]{2,1,0:T(8,128)(2,1)}, bf16[64,64,512]{2,1,0:T(8,128)(2,1)}) fusion(bf16[64,2,64,512]{3,2,1,0:T(8,128)(2,1)} %broadcast_multiply_fusion), kind=kLoop, calls=%fused_computation.14 | loop fusion | bytes 16777216 | tf_op jit(solution)/shard_map/squeeze | solution.py:65
  140.7 15.7 %copy.8 = bf16[64,64,512]{0,1,2:T(8,128)(2,1)} copy(bf16[64,64,512]{2,1,0:T(8,128)(2,1)} %get-tuple-element.8) | data formatting | bytes 8388608 | tf_op jit(solution)/shard_map/squeeze | solution.py:65
  156.4 2.9 %copy.7 = bf16[16,64,512]{1,0,2:T(8,128)(2,1)} copy(bf16[16,64,512]{2,1,0:T(8,128)(2,1)S(1)} %get-tuple-element.11) | data formatting | bytes 2097152 | tf_op jit(solution)/shard_map/squeeze | solution.py:65
  159.2 15.6 %copy.5 = bf16[64,64,512]{0,1,2:T(8,128)(2,1)} copy(bf16[64,64,512]{2,1,0:T(8,128)(2,1)} %get-tuple-element.7) | data formatting | bytes 8388608 | tf_op jit(solution)/shard_map/squeeze | solution.py:65
  174.9 0.0 copy-start
  174.9 7.9 %fusion.34 = f32[512,16,64]{2,1,0:T(8,128)} fusion(bf16[16,64,512]{1,0,2:T(8,128)(2,1)S(1)} %copy.4, bf16[64,64,512]{0,1,2:T(8,128)(2,1)} %copy.8), kind=kOutput, calls=%fused_computation.62 | convolution fusion | flops 67108864 | bytes 7340032 | tf_op jit(solution)/shard_map/dot_general | solution.py:32
  182.7 0.0 copy-done
  182.7 0.0 copy-start.1
  182.7 0.0 slice-start
  182.7 3.9 %fusion.32 = f32[512,16,64]{2,1,0:T(8,128)} fusion(bf16[16,64,512]{1,0,2:T(8,128)(2,1)S(1)} %copy.4, bf16[64,64,512]{0,1,2:T(8,128)(2,1)S(1)} %copy-done), kind=kOutput, calls=%fused_computation.60 | convolution fusion | flops 67108864 | bytes 7340032 | tf_op jit(solution)/shard_map/dot_general | solution.py:32
  186.6 0.0 copy-done.1
  186.6 0.0 slice-start.1
  186.6 3.7 %fusion.35 = f32[512,16,64]{2,1,0:T(8,128)} fusion(bf16[16,64,512]{1,0,2:T(8,128)(2,1)S(1)} %copy-done.1, bf16[64,64,512]{0,1,2:T(8,128)(2,1)S(1)} %copy-done), kind=kOutput, calls=%fused_computation.63 | convolution fusion | flops 67108864 | bytes 7340032 | tf_op jit(solution)/shard_map/dot_general | solution.py:32
  190.3 0.0 slice-done
  190.3 0.0 slice-done.1
  190.3 4.0 %fusion.33 = f32[512,16,64]{2,1,0:T(8,128)} fusion(bf16[16,64,512]{1,0,2:T(8,128)(2,1)S(1)} %copy-done.1, bf16[64,64,512]{0,1,2:T(8,128)(2,1)S(1)} %bitcast.30), kind=kOutput, calls=%fused_computation.61 | convolution fusion | flops 67108864 | bytes 7340032 | tf_op jit(solution)/shard_map/dot_general | solution.py:32
  194.3 2.8 %copy.10 = f32[512,16,64]{0,2,1:T(8,128)S(1)} copy(f32[512,16,64]{2,1,0:T(8,128)} %fusion.34) | data formatting | bytes 4194304 | tf_op jit(solution)/shard_map/dot_general | solution.py:32
  197.2 3.8 %copy.11 = f32[512,16,64]{0,2,1:T(8,128)} copy(f32[512,16,64]{2,1,0:T(8,128)} %fusion.35) | data formatting | bytes 4194304 | tf_op jit(solution)/shard_map/dot_general | solution.py:32
  201.0 3.8 %copy.6 = f32[512,16,64]{0,2,1:T(8,128)} copy(f32[512,16,64]{2,1,0:T(8,128)} %fusion.32) | data formatting | bytes 4194304 | tf_op jit(solution)/shard_map/dot_general | solution.py:32
  204.8 3.8 %copy.9 = f32[512,16,64]{0,2,1:T(8,128)} copy(f32[512,16,64]{2,1,0:T(8,128)} %fusion.33) | data formatting | bytes 4194304 | tf_op jit(solution)/shard_map/dot_general | solution.py:32
  208.6 8.7 %multiply_convert_fusion = (bf16[512,1024]{1,0:T(8,128)(2,1)S(1)}, bf16[512,1024]{1,0:T(8,128)(2,1)S(1)}) fusion(f32[512]{0:T(512)S(1)} %fusion.28, f32[512]{0:T(512)S(1)} %select_multiply_fusion), kind=kLoop, calls=%fused_computation.29 | loop fusion | flops 9437184 | bytes 2101248 | tf_op jit(solution)/shard_map/convert.1
  217.3 4.0 %multiply_convert_fusion.2 = (bf16[512,16,64]{0,2,1:T(8,128)(2,1)S(1)}, bf16[512,16,64]{0,2,1:T(8,128)(2,1)S(1)}) fusion(f32[512,16,64]{0,2,1:T(8,128)S(1)} %copy.10, f32[512,16,64]{0,2,1:T(8,128)} %copy.11, f32[512,16,64]{0,2,1:T(8,128)} %copy.6, f32[512,16,64]{0,2,1:T(8,128)} %copy.9), kind=kLoop, calls=%fused_computation.33 | loop fusion | flops 3145728 | bytes 10485760 | tf_op jit(solution)/shard_map/convert.3
  221.3 2.3 fusion.10
  223.6 0.1 fusion.31
  223.7 4.5 %collective-permute-start = (f32[16,2,1024]{2,1,0:T(2,128)S(1)}, f32[16,2,1024]{2,1,0:T(2,128)S(1)}, u32[]{:S(2)}, u32[]{:S(2)}) collective-permute-start(f32[16,2,1024]{2,1,0:T(2,128)S(1)} %get-tuple-element.9), channel_id=1, source_target_pairs={{0,1},{1,2},{2,3},{3,4},{4,5},{5,6},{6,7},{7,8},{8,9},{9,10},{10,1... | collective-permute-start | bytes 393224 | tf_op jit(solution)/shard_map/ppermute | solution.py:14
  228.2 1.3 collective-permute-start.1
  229.5 0.0 collective-permute-done
  229.5 1.9 collective-permute-done.1
  231.5 3.5 %fusion.3 = f32[16,64,1024]{2,1,0:T(8,128)} fusion(f32[16,64,1024]{2,1,0:T(8,128)S(1)} %fusion.10, f32[16,2,1024]{2,1,0:T(2,128)S(1)} %collective-permute-done.1, f32[16,2,1024]{2,1,0:T(2,128)S(1)} %collective-permute-done), kind=kLoop, calls=%fused_computation.7 | loop fusion | flops 9437184 | bytes 8650752 | tf_op jit(solution)/shard_map/div | solution.py:74
  (4 shorter events, 0.0 us)
Async XLA Ops:
  1.3 11.8 %copy-start.2 = (s32[64,64]{1,0:T(8,128)S(1)}, s32[64,64]{1,0:T(8,128)}, u32[]{:S(2)}) copy-start(s32[64,64]{1,0:T(8,128)} %param.4) | copy-start | bytes 49156
  174.9 7.9 %copy-start = (bf16[64,64,512]{0,1,2:T(8,128)(2,1)S(1)}, bf16[64,64,512]{0,1,2:T(8,128)(2,1)}, u32[]{:S(2)}) copy-start(bf16[64,64,512]{0,1,2:T(8,128)(2,1)} %copy.5) | copy-start | bytes 12582916
  182.7 3.9 %copy-start.1 = (bf16[16,64,512]{1,0,2:T(8,128)(2,1)S(1)}, bf16[16,64,512]{1,0,2:T(8,128)(2,1)}, u32[]{:S(2)}) copy-start(bf16[16,64,512]{1,0,2:T(8,128)(2,1)} %copy.7) | copy-start | bytes 3145732
  182.7 7.6 %slice-start = ((s8[8388608]{0:T(1024)(128)(4,1)}), s8[4194304]{0:T(1024)(128)(4,1)S(1)}, s32[]{:S(2)}) async-start(s8[8388608]{0:T(1024)(128)(4,1)} %bitcast.29), calls=%async_computation | async-start | bytes 8388608
  186.6 3.7 %slice-start.1 = ((s8[8388608]{0:T(1024)(128)(4,1)}), s8[4194304]{0:T(1024)(128)(4,1)S(1)}, s32[]{:S(2)}) async-start(s8[8388608]{0:T(1024)(128)(4,1)} %bitcast.29), calls=%async_computation.1 | async-start | bytes 8388608
  223.7 5.8 %collective-permute-start = (f32[16,2,1024]{2,1,0:T(2,128)S(1)}, f32[16,2,1024]{2,1,0:T(2,128)S(1)}, u32[]{:S(2)}, u32[]{:S(2)}) collective-permute-start(f32[16,2,1024]{2,1,0:T(2,128)S(1)} %get-tuple-element.9), channel_id=1, source_target_pairs={{0,1},{1,2},{2,3},{3,4},{4,5},{5,6},{6,7},{7,8},{8,9},{9,10},{10,1... | collective-permute-start | bytes 393224 | tf_op jit(solution)/shard_map/ppermute | solution.py:14
  228.2 3.2 %collective-permute-start.1 = (f32[16,2,1024]{2,1,0:T(2,128)S(1)}, f32[16,2,1024]{2,1,0:T(2,128)S(1)}, u32[]{:S(2)}, u32[]{:S(2)}) collective-permute-start(f32[16,2,1024]{2,1,0:T(2,128)S(1)} %get-tuple-element.10), channel_id=1, source_target_pairs={{1,0},{2,1},{3,2},{4,3},{5,4},{6,5},{7,6},{8,7},{9,8},{10,9},{11,1... | collective-permute-start | bytes 393224 | tf_op jit(solution)/shard_map/ppermute | solution.py:15
where the time goes:
time: 238 us; the launch traced here: 235 us
  blocking collectives  102 us (43%)
  local copies, waits for them, and re-layouts  71.2 us (30%)
  matrix products  28.6 us (12%)
  other arithmetic  24.9 us (10%)
  starting transfers between devices  5.79 us (2%)
    psum x1, blocking collectives, local(): got, got_valid = lax.psum((picked, picked_valid), 'chan')  102 us
    squeeze x2, local copies, waits for them, and re-layouts, local(): chan_m[:, 0]  21.7 us
    dot_general x4, matrix products, contract(): lax.dot_general(left, right, (((1,), (1,)), ((2,), (2,))), preferred_elem...  19.4 us
    squeeze x1, local copies, waits for them, and re-layouts, local(): chan_m[:, 1]  15.7 us
    dot_general x4, local copies, waits for them, and re-layouts, contract(): lax.dot_general(left, right, (((1,), (1,)), ((2,), (2,))), preferred_elem...  14.3 us
    another operation x2, other arithmetic  12.6 us
    unnamed x12, local copies, waits for them, and re-layouts  12.5 us
    mul x1, other arithmetic, local(): chan_m = spectra * chan_valid.astype(jnp.bfloat16)[:, None, :, None]  7.22 us
  transfers between devices with their start and end apart: 2, of which 1 were waited for; matrix products, arithmetic and copies ran while one was open for 0% of the time, Pallas kernels for 0%

commit v1 on v0

v1 whole, which is shorter than its diff:
```python
import functools

import jax
import jax.numpy as jnp
import numpy as np
from jax import lax
from jax.experimental import pallas as pl
from jax.experimental.pallas import tpu as pltpu
from jax.sharding import PartitionSpec as P

MESH = pl.DeviceIdType.MESH
HALO = 2


def make_table(nbins, nlags):
    freq = np.arange(nbins, dtype=np.int64)
    phase = (freq[:, None] * np.arange(nlags, dtype=np.int64)[None, :]) % nlags
    angle = 2.0 * np.pi * phase / nlags
    weight = np.where(freq == 0, 1.0, 2.0) / nlags
    table = np.concatenate([weight[:, None] * np.cos(angle), -weight[:, None] * np.sin(angle)])
    return table.astype(np.float32).astype(jnp.bfloat16)


def pick_kernel(nsrc, src_ref, mask_ref, spec_ref, out_ref, buf, sems):
    nchan = spec_ref.shape[0]
    me = lax.axis_index("chan")
    spots, copies = [], []
    for row in range(nsrc + 2 * HALO):
        if row < nsrc:
            spot = src_ref[row] - me * nchan
        else:
            spot = row - nsrc if row < nsrc + HALO else nchan - 2 * HALO + row - nsrc
        held = jnp.clip(spot, 0, nchan - 1) if row < nsrc else spot
        copy = pltpu.make_async_copy(spec_ref.at[held], buf.at[row], sems.at[row])
        copy.start()
        spots.append(spot)
        copies.append(copy)
    mask = mask_ref[...]
    lane = lax.broadcasted_iota(jnp.int32, mask.shape, 1)
    for row, (spot, copy) in enumerate(zip(spots, copies)):
        column = jnp.sum(jnp.where(lane == spot, mask, 0.0), axis=1, keepdims=True)
        copy.wait()
        out_ref[row] = (buf[row].astype(jnp.float32) * column).astype(out_ref.dtype)


def share_kernel(outer, inner, nchunk, pick_ref, edge_ref, out_ref, halo_ref, part, first, second,
                 ins, outs, send_sem, recv_sem, edge_send, edge_recv):
    half = nchunk // 2
    size = outer * inner * 2
    me = lax.axis_index("chan")
    core, chip = me % 2, me // 2
    j, i = chip % inner, chip // inner
    lines = ((j, inner, 2), (i, outer, 2 * inner))
    partner = me + 1 - 2 * core

    barrier = pltpu.get_barrier_semaphore()

    def greet(there):
        pl.semaphore_signal(barrier, inc=1, device_id={"chan": there}, device_id_type=MESH)

    greet(partner)
    count = jnp.int32(1)
    for pos, length, stride in lines + ((me, size, 1),):
        @pl.when(pos > 0)
        def _():
            greet(me - stride)

        @pl.when(pos < length - 1)
        def _():
            greet(me + stride)

        count = count + (pos > 0).astype(jnp.int32) + (pos < length - 1).astype(jnp.int32)
    pl.semaphore_wait(barrier, count)

    def remote(src, dst, kind, k, there):
        return pltpu.make_async_remote_copy(
            src_ref=src, dst_ref=dst, send_sem=send_sem.at[kind, k], recv_sem=recv_sem.at[kind, k],
            device_id={"chan": there}, device_id_type=MESH)

    def across(k):
        return remote(pick_ref.at[(1 - core) * half + k], part.at[k], 0, k, partner)

    def back(k):
        spot = core * half + k
        return remote(out_ref.at[spot], out_ref.at[spot], 1, k, partner)

    def hop(line, up, src, k):
        pos, length, stride = lines[line]
        kind = 2 + 2 * line + (0 if up else 1)
        there = me + stride if up else me - stride
        return remote(src, ins.at[kind - 2, k], kind, k, there)

    def to_after():
        return pltpu.make_async_remote_copy(
            src_ref=edge_ref.at[pl.ds(HALO, HALO)], dst_ref=halo_ref.at[pl.ds(0, HALO)],
            send_sem=edge_send.at[0], recv_sem=edge_recv.at[0],
            device_id={"chan": me + 1}, device_id_type=MESH)

    def to_before():
        return pltpu.make_async_remote_copy(
            src_ref=edge_ref.at[pl.ds(0, HALO)], dst_ref=halo_ref.at[pl.ds(HALO, HALO)],
            send_sem=edge_send.at[1], recv_sem=edge_recv.at[1],
            device_id={"chan": me - 1}, device_id_type=MESH)

    def begin(line, x, k):
        pos, length, _ = lines[line]
        if length == 1:
            return

        @pl.when(pos == 0)
        def _():
            hop(line, True, x.at[k], k).start()

        @pl.when(pos == length - 1)
        def _():
            hop(line, False, x.at[k], k).start()

    def finish(line, x, k, total, at):
        pos, length, _ = lines[line]
        if length == 1:
            total[at] = x[k]
            return
        low, high = ins.at[2 * line], ins.at[2 * line + 1]

        @pl.when(pos > 0)
        def _():
            hop(line, True, x.at[k], k).wait_recv()
            if length > 2:
                @pl.when(pos < length - 1)
                def _():
                    outs[2 * line, k] = x[k] + low[k]
                    hop(line, True, outs.at[2 * line, k], k).start()

        @pl.when(pos < length - 1)
        def _():
            hop(line, False, x.at[k], k).wait_recv()
            if length > 2:
                @pl.when(pos > 0)
                def _():
                    outs[2 * line + 1, k] = x[k] + high[k]
                    hop(line, False, outs.at[2 * line + 1, k], k).start()

        @pl.when(pos == 0)
        def _():
            total[at] = x[k] + high[k]

        @pl.when(pos == length - 1)
        def _():
            total[at] = x[k] + low[k]

        if length > 2:
            @pl.when((pos > 0) & (pos < length - 1))
            def _():
                total[at] = x[k] + low[k] + high[k]

    def send_across(k, carry):
        across(k).start()
        return carry

    lax.fori_loop(0, half, send_across, 0)

    @pl.when(me < size - 1)
    def _():
        to_after().start()

    @pl.when(me > 0)
    def _():
        to_before().start()

    @pl.when(me == 0)
    def _():
        halo_ref[0:HALO] = jnp.zeros((HALO,) + halo_ref.shape[1:], halo_ref.dtype)

    @pl.when(me == size - 1)
    def _():
        halo_ref[HALO:] = jnp.zeros((HALO,) + halo_ref.shape[1:], halo_ref.dtype)

    def step(t, carry):
        @pl.when(t < half)
        def _():
            across(t).wait_recv()
            first[t] = pick_ref[core * half + t] + part[t]
            begin(0, first, t)

        @pl.when((t >= 1) & (t < half + 1))
        def _():
            finish(0, first, t - 1, second, t - 1)
            begin(1, second, t - 1)

        @pl.when(t >= 2)
        def _():
            finish(1, second, t - 2, out_ref, core * half + t - 2)
            back(t - 2).start()

        return carry

    lax.fori_loop(0, half + 2, step, 0)

    def close(k, carry):
        across(k).wait_send()
        other = (1 - core) * half + k
        remote(out_ref.at[other], out_ref.at[other], 1, k, partner).wait_recv()
        back(k).wait_send()
        for line, (pos, length, _) in enumerate(lines):
            if length == 1:
                continue

            @pl.when(pos < length - 1)
            def _():
                hop(line, True, first.at[k], k).wait_send()

            @pl.when(pos > 0)
            def _():
                hop(line, False, first.at[k], k).wait_send()

        return carry

    lax.fori_loop(0, half, close, 0)

    @pl.when(me < size - 1)
    def _():
        to_after().wait_send()
        to_before().wait_recv()

    @pl.when(me > 0)
    def _():
        to_before().wait_send()
        to_after().wait_recv()


def lag_kernel(nwin, nrow, sgroup, spec_ref, valid_ref, src_ref, halo_ref, table_ref, out_ref,
               chan_t, src_t, cross_t, lag):
    nchan, depth, fb = spec_ref.shape
    nsrc = src_ref.shape[0]
    nbins = table_ref.shape[0] // 2
    steps = nbins // fb
    at = pl.program_id(0)

    @pl.when(at < steps)
    def _():
        def turn(x):
            return jnp.transpose(x).astype(jnp.float32)

        for c in range(HALO):
            chan_t[c * fb:(c + 1) * fb] = turn(halo_ref[c])
            far = nchan + HALO + c
            chan_t[far * fb:(far + 1) * fb] = turn(halo_ref[HALO + c])

        def channel(c, carry):
            chan_t[pl.ds(pl.multiple_of((c + HALO) * fb, fb), fb)] = (
                turn(spec_ref[c]) * valid_ref[pl.ds(c, 1)])
            return carry

        lax.fori_loop(0, nchan, channel, 0, unroll=4)
        sign = jnp.where(lax.broadcasted_iota(jnp.int32, (1, depth), 1) < nwin, -1.0, 1.0)

        def source(s, carry):
            x = turn(src_ref[s])
            src_t[pl.ds(pl.multiple_of(s * fb, fb), fb)] = x
            src_t[pl.ds(pl.multiple_of((s + nsrc) * fb, fb), fb)] = (
                pltpu.roll(x, nwin, axis=1) * sign)
            return carry

        lax.fori_loop(0, nsrc, source, 0, unroll=2)

        def one(f, carry):
            right = chan_t[pl.ds(f, nrow, stride=fb)].astype(jnp.bfloat16)
            left = src_t[pl.ds(f, 2 * nsrc, stride=fb)].astype(jnp.bfloat16)
            both = lax.dot_general(left, right, (((1,), (1,)), ((), ())),
                                   preferred_element_type=jnp.float32)
            row = pl.multiple_of((at * fb + f) * 2 * nsrc, 2 * nsrc)
            cross_t[pl.ds(row, 2 * nsrc), 0:nrow] = both * (1.0 / nwin)
            return carry

        lax.fori_loop(0, fb, one, 0, unroll=8)

    @pl.when(at >= steps)
    def _():
        group = at - steps
        rows = []
        for q in range(sgroup):
            s = group * sgroup + q
            re = cross_t[pl.ds(s, nbins, stride=2 * nsrc)]
            im = cross_t[pl.ds(s + nsrc, nbins, stride=2 * nsrc)]
            flat = jnp.concatenate([re, im], axis=0).astype(jnp.bfloat16)
            rows.append(jnp.transpose(flat)[0:nrow])
        lag[...] = jnp.dot(jnp.concatenate(rows, axis=0), table_ref[...],
                           preferred_element_type=jnp.float32)
        for q in range(sgroup):
            base = q * nrow
            total = lag[base:base + nchan] + lag[base + 1:base + 1 + nchan]
            for k in range(2, 2 * HALO + 1):
                total = total + lag[base + k:base + k + nchan]
            out_ref[q] = total / (2 * HALO + 1.0)


def local(size, spectra, valid, sources):
    nchan, _, nwin, nbins = spectra.shape
    nsrc = sources.shape[0]
    depth, nlags = 2 * nwin, 2 * nbins
    spec = spectra.reshape(nchan, depth, nbins)
    flags = valid.astype(jnp.float32)
    flags2 = jnp.concatenate([flags, flags], axis=1)
    vmem = pl.BlockSpec(memory_space=pltpu.VMEM)

    picked = pl.pallas_call(
        functools.partial(pick_kernel, nsrc),
        out_shape=jax.ShapeDtypeStruct((nsrc + 2 * HALO, depth, nbins), jnp.bfloat16),
        in_specs=[pl.BlockSpec(memory_space=pltpu.SMEM), vmem, pl.BlockSpec(memory_space=pl.ANY)],
        out_specs=vmem,
        scratch_shapes=[pltpu.VMEM((nsrc + 2 * HALO, depth, nbins), jnp.bfloat16),
                        pltpu.SemaphoreType.DMA((nsrc + 2 * HALO,))],
        compiler_params=pltpu.CompilerParams(vmem_limit_bytes=24 << 20),
        name="pick",
    )(sources, flags2.T, spec)

    chips = size // 2
    inner = 1
    while (2 * inner) ** 2 <= chips and chips % (2 * inner) == 0:
        inner *= 2
    outer = chips // inner
    cut = 2
    nchunk, crow = nsrc * cut, depth // cut
    half = nchunk // 2
    chunk = lambda *lead: pltpu.VMEM(lead + (crow, nbins), jnp.bfloat16)
    src, halo = pl.pallas_call(
        functools.partial(share_kernel, outer, inner, nchunk),
        out_shape=[jax.ShapeDtypeStruct((nchunk, crow, nbins), jnp.bfloat16),
                   jax.ShapeDtypeStruct((2 * HALO, depth, nbins), jnp.bfloat16)],
        in_specs=[vmem, vmem],
        out_specs=[vmem, vmem],
        scratch_shapes=[chunk(half), chunk(half), chunk(half), chunk(4, half), chunk(4, half),
                        pltpu.SemaphoreType.DMA((6, half)), pltpu.SemaphoreType.DMA((6, half)),
                        pltpu.SemaphoreType.DMA((2,)), pltpu.SemaphoreType.DMA((2,))],
        compiler_params=pltpu.CompilerParams(
            collective_id=0, has_side_effects=True, vmem_limit_bytes=40 << 20),
        name="share",
    )(picked[:nsrc].reshape(nchunk, crow, nbins), picked[nsrc:])
    src = src.reshape(nsrc, depth, nbins)

    fb = 128
    steps = nbins // fb
    sgroup = 4 if nsrc % 4 == 0 else 1
    nrow = -(-(nchan + 2 * HALO) // 16) * 16
    by_f = lambda at: (0, 0, jnp.minimum(at, steps - 1))
    return pl.pallas_call(
        functools.partial(lag_kernel, nwin, nrow, sgroup),
        grid=(steps + nsrc // sgroup,),
        out_shape=jax.ShapeDtypeStruct((nsrc, nchan, nlags), jnp.float32),
        in_specs=[pl.BlockSpec((nchan, depth, fb), by_f),
                  pl.BlockSpec((nchan, depth), lambda at: (0, 0)),
                  pl.BlockSpec((nsrc, depth, fb), by_f),
                  pl.BlockSpec((2 * HALO, depth, fb), by_f),
                  pl.BlockSpec((nlags, nlags), lambda at: (0, 0))],
        out_specs=pl.BlockSpec((sgroup, nchan, nlags), lambda at: (jnp.maximum(at - steps, 0), 0, 0)),
        scratch_shapes=[pltpu.VMEM((nrow * fb, depth), jnp.float32),
                        pltpu.VMEM((2 * nsrc * fb, depth), jnp.float32),
                        pltpu.VMEM((nbins * 2 * nsrc, 128), jnp.float32),
                        pltpu.VMEM((sgroup * nrow, nlags), jnp.float32)],
        compiler_params=pltpu.CompilerParams(vmem_limit_bytes=56 << 20),
        name="lags",
    )(spec, flags2, src, halo, jnp.asarray(make_table(nbins, nlags)))


def solution(mesh):
    in_specs = (P(("grp", "chan"), None, None, None), P(("grp", "chan"), None), P("grp"))
    out_specs = P("grp", "chan", None)
    return jax.shard_map(functools.partial(local, mesh.shape["chan"]), mesh=mesh,
                         in_specs=in_specs, out_specs=out_specs, check_vma=False)
```

time: 238 us -> 194 us (0.82); the launches traced: 235 us -> 194 us
  Pallas kernels: 0 us -> 186 us
  blocking collectives: 102 us -> 0 us
  local copies, waits for them, and re-layouts: 71.2 us -> 6.42 us
  matrix products: 28.6 us -> 0 us
  other arithmetic: 24.9 us -> 1.44 us
  starting transfers between devices: 5.79 us -> 0 us
    pallas_call x0 -> x3, Pallas kernels: none -> 186 us  [the longest x1 130 us: local(): pl.pallas_call(functools.partial(share_kernel, outer, inner, nchunk), out...]
    psum x1 -> x0, blocking collectives: 102 us -> none  [local(): got, got_valid = lax.psum((picked, picked_valid), 'chan')]
    squeeze x6 -> x0, local copies, waits for them, and re-layouts: 44.3 us -> none  [the longest x2 21.7 us: local(): chan_m[:, 0]]
    dot_general x7 -> x0, matrix products: 28.6 us -> none  [the longest x4 19.4 us: contract(): lax.dot_general(left, right, (((1,), (1,)), ((2,), (2,))), preferred_elem...]
    dot_general x4 -> x0, local copies, waits for them, and re-layouts: 14.3 us -> none  [contract(): lax.dot_general(left, right, (((1,), (1,)), ((2,), (2,))), preferred_elem...]
    another operation x2 -> x0, other arithmetic: 12.6 us -> none
    mul x2 -> x0, other arithmetic: 7.42 us -> none  [the longest x1 7.22 us: local(): chan_m = spectra * chan_valid.astype(jnp.bfloat16)[:, None, :, None]]
    unnamed x12 -> x8, local copies, waits for them, and re-layouts: 12.5 us -> 6.16 us
  transfers between devices with their start and end apart: 2 -> 0, of which waited for: 1 -> 0; matrix products, arithmetic and copies ran while one was open for 0% -> 0% of each run, Pallas kernels for 0% -> 0%
where the time goes in v1:
time: 194 us
  Pallas kernels  186 us (96%)
  local copies, waits for them, and re-layouts  6.42 us (3%)
    pallas_call x1, Pallas kernels, local(): pl.pallas_call(functools.partial(share_kernel, outer, inner, nchunk), out...  130 us
    pallas_call x1, Pallas kernels, local(): pl.pallas_call(functools.partial(lag_kernel, nwin, nrow, sgroup), grid=(s...  49.6 us
    unnamed x8, local copies, waits for them, and re-layouts  6.16 us
    pallas_call x1, Pallas kernels, local(): pl.pallas_call(functools.partial(pick_kernel, nsrc), out_shape=jax.ShapeD...  6.08 us

profile of v1, /device:TPU:0, one launch (start us, length us, event | category | flops | bytes accessed | tf_op | source)
XLA Modules:
  0.0 193.6 jit_solution(16511456738923065727)
XLA Ops:
  0.0 0.8 convert_element_type.3
  0.8 0.7 fusion
  1.4 0.1 copy.5.mask_ref
  1.5 0.0 copy-start
  1.6 3.4 %copy-done = bf16[64,2,64,512]{3,2,1,0:T(8,128)(2,1)S(1)} copy-done((bf16[64,2,64,512]{3,2,1,0:T(8,128)(2,1)S(1)}, bf16[64,2,64,512]{3,2,1,0:T(8,128)(2,1)}, u32[]{:S(2)}) %copy-start) | copy-done | bytes 8388632
  4.9 0.0 copy-start.3
  4.9 0.7 copy-done.3
  5.6 6.1 %pick.1 = bf16[20,128,512]{2,1,0:T(8,128)(2,1)S(1)} custom-call(s32[16]{0:T(128)S(1)} %copy-done.3, f32[128,64]{1,0:T(8,128)S(1)} %copy.5.mask_ref, bf16[64,128,512]{2,1,0:T(8,128)(2,1)S(1)} %bitcast.6), custom_call_target="tpu_custom_call" | custom-call | tf_op jit(solution)/shard_map/pick/pallas_call | solution.py:306
  11.7 0.1 slice.8
  11.9 130.0 %share.1 = (bf16[32,64,512]{2,1,0:T(8,128)(2,1)S(1)}, bf16[4,128,512]{2,1,0:T(8,128)(2,1)S(1)}) custom-call(bf16[32,64,512]{2,1,0:T(8,128)(2,1)S(1)} %bitcast.7, bf16[4,128,512]{2,1,0:T(8,128)(2,1)S(1)} %slice.9.edge_ref), custom_call_target="tpu_custom_call" | custom-call | tf_op jit(solution)/shard_map/share/pallas_call | solution.py:326
  141.8 0.0 copy-start.1
  141.8 1.3 copy-done.1
  143.2 0.0 copy-start.2
  143.2 0.8 copy-done.2
  144.0 49.6 %lags.1 = f32[16,64,1024]{2,1,0:T(8,128)} custom-call(bf16[64,128,512]{2,1,0:T(8,128)(2,1)} %bitcast.5, f32[64,128]{1,0:T(8,128)} %get-tuple-element.10.valid_ref, bf16[16,128,512]{2,1,0:T(8,128)(2,1)} %bitcast.8, bf16[4,128,512]{2,1,0:T(8,128)(2,1)} %copy-done.2, bf16[1024,1024]{1,0:T(8,128)(2,1)} %constant.2.clone.table_ref), custom_call_target="tpu_custom_call" | custom-call | tf_op jit(solution)/shard_map/lags/pallas_call | solution.py:346
  (1 shorter events, 0.0 us)
Async XLA Ops:
  1.5 3.4 %copy-start = (bf16[64,2,64,512]{3,2,1,0:T(8,128)(2,1)S(1)}, bf16[64,2,64,512]{3,2,1,0:T(8,128)(2,1)}, u32[]{:S(2)}) copy-start(bf16[64,2,64,512]{3,2,1,0:T(8,128)(2,1)} %param.4) | copy-start | bytes 25165828
  4.9 0.7 copy-start.3
  141.8 1.3 copy-start.1
  143.2 0.8 copy-start.2

commit v2 on v1

--- a/solution.py
+++ b/solution.py
@@ -10,6 +10,7 @@
 
 MESH = pl.DeviceIdType.MESH
 HALO = 2
+LAG = 2
 
 
 def make_table(nbins, nlags):
@@ -115,6 +116,42 @@
         def _():
             hop(line, False, x.at[k], k).start()
 
+    def guarded(k, also, run):
+        @pl.when((k >= 0) & (k < half) & also)
+        def _():
+            run(k)
+
+    def relay(line, x, t):
+        pos, length, _ = lines[line]
+        if length == 1:
+            return
+
+        def go(up):
+            kind = 2 * line + (0 if up else 1)
+            behind = pos - 1 if up else length - 2 - pos
+            last = pos == (length - 1 if up else 0)
+            first_one = pos == (0 if up else length - 1)
+
+            def run(k):
+                hop(line, up, x.at[k], k).wait_recv()
+                if length > 2:
+                    @pl.when(jnp.logical_not(last))
+                    def _():
+                        outs[kind, k] = x[k] + ins[kind, k]
+                        hop(line, up, outs.at[kind, k], k).start()
+
+            guarded(t - LAG * behind, jnp.logical_not(first_one), run)
+
+        @pl.when(2 * pos < length)
+        def _():
+            go(True)
+            go(False)
+
+        @pl.when(2 * pos >= length)
+        def _():
+            go(False)
+            go(True)
+
     def finish(line, x, k, total, at):
         pos, length, _ = lines[line]
         if length == 1:
@@ -122,24 +159,6 @@
             return
         low, high = ins.at[2 * line], ins.at[2 * line + 1]
 
-        @pl.when(pos > 0)
-        def _():
-            hop(line, True, x.at[k], k).wait_recv()
-            if length > 2:
-                @pl.when(pos < length - 1)
-                def _():
-                    outs[2 * line, k] = x[k] + low[k]
-                    hop(line, True, outs.at[2 * line, k], k).start()
-
-        @pl.when(pos < length - 1)
-        def _():
-            hop(line, False, x.at[k], k).wait_recv()
-            if length > 2:
-                @pl.when(pos > 0)
-                def _():
-                    outs[2 * line + 1, k] = x[k] + high[k]
-                    hop(line, False, outs.at[2 * line + 1, k], k).start()
-
         @pl.when(pos == 0)
         def _():
             total[at] = x[k] + high[k]
@@ -175,26 +194,33 @@
     def _():
         halo_ref[HALO:] = jnp.zeros((HALO,) + halo_ref.shape[1:], halo_ref.dtype)
 
+    ready = LAG
+    passed = ready + LAG * max(inner - 2, 0)
+    reached = passed + LAG
+    done = reached + LAG * max(outer - 2, 0)
+
     def step(t, carry):
-        @pl.when(t < half)
-        def _():
-            across(t).wait_recv()
-            first[t] = pick_ref[core * half + t] + part[t]
-            begin(0, first, t)
-
-        @pl.when((t >= 1) & (t < half + 1))
-        def _():
-            finish(0, first, t - 1, second, t - 1)
-            begin(1, second, t - 1)
-
-        @pl.when(t >= 2)
-        def _():
-            finish(1, second, t - 2, out_ref, core * half + t - 2)
-            back(t - 2).start()
-
+        def enter(k):
+            across(k).wait_recv()
+            first[k] = pick_ref[core * half + k] + part[k]
+            begin(0, first, k)
+
+        def turn(k):
+            finish(0, first, k, second, k)
+            begin(1, second, k)
+
+        def leave(k):
+            finish(1, second, k, out_ref, core * half + k)
+            back(k).start()
+
+        guarded(t, True, enter)
+        relay(0, first, t - ready)
+        guarded(t - passed, True, turn)
+        relay(1, second, t - reached)
+        guarded(t - done, True, leave)
         return carry
 
-    lax.fori_loop(0, half + 2, step, 0)
+    lax.fori_loop(0, half + done, step, 0)
 
     def close(k, carry):
         across(k).wait_send()

time: 194 us -> 116 us (0.60)
  Pallas kernels: 186 us -> 108 us
    pallas_call x1, Pallas kernels: 130 us -> 51.8 us  [local(): pl.pallas_call(functools.partial(share_kernel, outer, inner, nchunk), out...]
where the time goes in v2:
time: 116 us; the launch traced here: 115 us
  Pallas kernels  108 us (93%)
  local copies, waits for them, and re-layouts  6.42 us (6%)
  other arithmetic  1.44 us (1%)
    pallas_call x1, Pallas kernels, local(): pl.pallas_call(functools.partial(share_kernel, outer, inner, nchunk), out...  51.8 us
    pallas_call x1, Pallas kernels, local(): pl.pallas_call(functools.partial(lag_kernel, nwin, nrow, sgroup), grid=(s...  49.6 us
    unnamed x8, local copies, waits for them, and re-layouts  6.16 us
    pallas_call x1, Pallas kernels, local(): pl.pallas_call(functools.partial(pick_kernel, nsrc), out_shape=jax.ShapeD...  6.08 us

profile of v2, /device:TPU:0, one launch (start us, length us, event | category | flops | bytes accessed | tf_op | source)
XLA Modules:
  0.0 115.4 jit_solution(18071336905098065262)
XLA Ops:
  0.0 0.8 convert_element_type.3
  0.8 0.7 fusion
  1.4 0.1 copy.5.mask_ref
  1.5 0.0 copy-start
  1.6 3.4 %copy-done = bf16[64,2,64,512]{3,2,1,0:T(8,128)(2,1)S(1)} copy-done((bf16[64,2,64,512]{3,2,1,0:T(8,128)(2,1)S(1)}, bf16[64,2,64,512]{3,2,1,0:T(8,128)(2,1)}, u32[]{:S(2)}) %copy-start) | copy-done | bytes 8388632
  4.9 0.0 copy-start.3
  4.9 0.7 copy-done.3
  5.6 6.1 %pick.1 = bf16[20,128,512]{2,1,0:T(8,128)(2,1)S(1)} custom-call(s32[16]{0:T(128)S(1)} %copy-done.3, f32[128,64]{1,0:T(8,128)S(1)} %copy.5.mask_ref, bf16[64,128,512]{2,1,0:T(8,128)(2,1)S(1)} %bitcast.6), custom_call_target="tpu_custom_call" | custom-call | tf_op jit(solution)/shard_map/pick/pallas_call | solution.py:332
  11.7 0.1 slice.8
  11.9 51.8 %share.1 = (bf16[32,64,512]{2,1,0:T(8,128)(2,1)S(1)}, bf16[4,128,512]{2,1,0:T(8,128)(2,1)S(1)}) custom-call(bf16[32,64,512]{2,1,0:T(8,128)(2,1)S(1)} %bitcast.7, bf16[4,128,512]{2,1,0:T(8,128)(2,1)S(1)} %slice.9.edge_ref), custom_call_target="tpu_custom_call" | custom-call | tf_op jit(solution)/shard_map/share/pallas_call | solution.py:352
  63.7 0.0 copy-start.1
  63.7 1.3 %copy-done.1 = bf16[32,64,512]{2,1,0:T(8,128)(2,1)} copy-done((bf16[32,64,512]{2,1,0:T(8,128)(2,1)}, bf16[32,64,512]{2,1,0:T(8,128)(2,1)S(1)}, u32[]{:S(2)}) %copy-start.1) | copy-done | bytes 2097176
  65.0 0.0 copy-start.2
  65.0 0.8 copy-done.2
  65.8 49.6 %lags.1 = f32[16,64,1024]{2,1,0:T(8,128)} custom-call(bf16[64,128,512]{2,1,0:T(8,128)(2,1)} %bitcast.5, f32[64,128]{1,0:T(8,128)} %get-tuple-element.10.valid_ref, bf16[16,128,512]{2,1,0:T(8,128)(2,1)} %bitcast.8, bf16[4,128,512]{2,1,0:T(8,128)(2,1)} %copy-done.2, bf16[1024,1024]{1,0:T(8,128)(2,1)} %constant.2.clone.table_ref), custom_call_target="tpu_custom_call" | custom-call | tf_op jit(solution)/shard_map/lags/pallas_call | solution.py:372
  (1 shorter events, 0.0 us)
Async XLA Ops:
  1.5 3.4 %copy-start = (bf16[64,2,64,512]{3,2,1,0:T(8,128)(2,1)S(1)}, bf16[64,2,64,512]{3,2,1,0:T(8,128)(2,1)}, u32[]{:S(2)}) copy-start(bf16[64,2,64,512]{3,2,1,0:T(8,128)(2,1)} %param.4) | copy-start | bytes 25165828
  4.9 0.7 copy-start.3
  63.7 1.3 %copy-start.1 = (bf16[32,64,512]{2,1,0:T(8,128)(2,1)}, bf16[32,64,512]{2,1,0:T(8,128)(2,1)S(1)}, u32[]{:S(2)}) copy-start(bf16[32,64,512]{2,1,0:T(8,128)(2,1)S(1)} %get-tuple-element.7) | copy-start | bytes 6291460
  65.0 0.8 copy-start.2

commit v3 on v2

--- a/solution.py
+++ b/solution.py
@@ -22,7 +22,7 @@
     return table.astype(np.float32).astype(jnp.bfloat16)
 
 
-def pick_kernel(nsrc, src_ref, mask_ref, spec_ref, out_ref, buf, sems):
+def pick_kernel(nsrc, src_ref, mask_ref, spec_ref, out_ref, edge_ref, buf, sems):
     nchan = spec_ref.shape[0]
     me = lax.axis_index("chan")
     spots, copies = [], []
@@ -41,7 +41,11 @@
     for row, (spot, copy) in enumerate(zip(spots, copies)):
         column = jnp.sum(jnp.where(lane == spot, mask, 0.0), axis=1, keepdims=True)
         copy.wait()
-        out_ref[row] = (buf[row].astype(jnp.float32) * column).astype(out_ref.dtype)
+        masked = (buf[row].astype(jnp.float32) * column).astype(out_ref.dtype)
+        if row < nsrc:
+            out_ref[row] = masked
+        else:
+            edge_ref[row - nsrc] = masked
 
 
 def share_kernel(outer, inner, nchunk, pick_ref, edge_ref, out_ref, halo_ref, part, first, second,
@@ -261,6 +265,7 @@
     nbins = table_ref.shape[0] // 2
     steps = nbins // fb
     at = pl.program_id(0)
+    pitch, cpitch = fb + 1, 2 * nsrc + 1
 
     @pl.when(at < steps)
     def _():
@@ -268,12 +273,12 @@
             return jnp.transpose(x).astype(jnp.float32)
 
         for c in range(HALO):
-            chan_t[c * fb:(c + 1) * fb] = turn(halo_ref[c])
+            chan_t[c * pitch:c * pitch + fb] = turn(halo_ref[c])
             far = nchan + HALO + c
-            chan_t[far * fb:(far + 1) * fb] = turn(halo_ref[HALO + c])
+            chan_t[far * pitch:far * pitch + fb] = turn(halo_ref[HALO + c])
 
         def channel(c, carry):
-            chan_t[pl.ds(pl.multiple_of((c + HALO) * fb, fb), fb)] = (
+            chan_t[pl.ds((c + HALO) * pitch, fb)] = (
                 turn(spec_ref[c]) * valid_ref[pl.ds(c, 1)])
             return carry
 
@@ -282,19 +287,19 @@
 
         def source(s, carry):
             x = turn(src_ref[s])
-            src_t[pl.ds(pl.multiple_of(s * fb, fb), fb)] = x
-            src_t[pl.ds(pl.multiple_of((s + nsrc) * fb, fb), fb)] = (
+            src_t[pl.ds(s * pitch, fb)] = x
+            src_t[pl.ds((s + nsrc) * pitch, fb)] = (
                 pltpu.roll(x, nwin, axis=1) * sign)
             return carry
 
         lax.fori_loop(0, nsrc, source, 0, unroll=2)
 
         def one(f, carry):
-            right = chan_t[pl.ds(f, nrow, stride=fb)].astype(jnp.bfloat16)
-            left = src_t[pl.ds(f, 2 * nsrc, stride=fb)].astype(jnp.bfloat16)
+            right = chan_t[pl.ds(f, nrow, stride=pitch)].astype(jnp.bfloat16)
+            left = src_t[pl.ds(f, 2 * nsrc, stride=pitch)].astype(jnp.bfloat16)
             both = lax.dot_general(left, right, (((1,), (1,)), ((), ())),
                                    preferred_element_type=jnp.float32)
-            row = pl.multiple_of((at * fb + f) * 2 * nsrc, 2 * nsrc)
+            row = (at * fb + f) * cpitch
             cross_t[pl.ds(row, 2 * nsrc), 0:nrow] = both * (1.0 / nwin)
             return carry
 
@@ -306,18 +311,21 @@
         rows = []
         for q in range(sgroup):
             s = group * sgroup + q
-            re = cross_t[pl.ds(s, nbins, stride=2 * nsrc)]
-            im = cross_t[pl.ds(s + nsrc, nbins, stride=2 * nsrc)]
+            re = cross_t[pl.ds(s, nbins, stride=cpitch)]
+            im = cross_t[pl.ds(s + nsrc, nbins, stride=cpitch)]
             flat = jnp.concatenate([re, im], axis=0).astype(jnp.bfloat16)
             rows.append(jnp.transpose(flat)[0:nrow])
-        lag[...] = jnp.dot(jnp.concatenate(rows, axis=0), table_ref[...],
-                           preferred_element_type=jnp.float32)
+        lags = jnp.dot(jnp.concatenate(rows, axis=0), table_ref[...],
+                       preferred_element_type=jnp.float32)
+        for n in range(lag.shape[0]):
+            lag[n] = lags[:, n * 128:(n + 1) * 128]
         for q in range(sgroup):
             base = q * nrow
-            total = lag[base:base + nchan] + lag[base + 1:base + 1 + nchan]
-            for k in range(2, 2 * HALO + 1):
-                total = total + lag[base + k:base + k + nchan]
-            out_ref[q] = total / (2 * HALO + 1.0)
+            for n in range(lag.shape[0]):
+                total = lag[n, base:base + nchan] + lag[n, base + 1:base + 1 + nchan]
+                for k in range(2, 2 * HALO + 1):
+                    total = total + lag[n, base + k:base + k + nchan]
+                out_ref[q, :, n * 128:(n + 1) * 128] = total / (2 * HALO + 1.0)
 
 
 def local(size, spectra, valid, sources):
@@ -329,14 +337,15 @@
     flags2 = jnp.concatenate([flags, flags], axis=1)
     vmem = pl.BlockSpec(memory_space=pltpu.VMEM)
 
-    picked = pl.pallas_call(
+    picked, edges = pl.pallas_call(
         functools.partial(pick_kernel, nsrc),
-        out_shape=jax.ShapeDtypeStruct((nsrc + 2 * HALO, depth, nbins), jnp.bfloat16),
-        in_specs=[pl.BlockSpec(memory_space=pltpu.SMEM), vmem, pl.BlockSpec(memory_space=pl.ANY)],
-        out_specs=vmem,
+        out_shape=[jax.ShapeDtypeStruct((nsrc, depth, nbins), jnp.bfloat16),
+                   jax.ShapeDtypeStruct((2 * HALO, depth, nbins), jnp.bfloat16)],
+        in_specs=[pl.BlockSpec(memory_space=pltpu.SMEM), vmem, pl.BlockSpec(memory_space=pltpu.MemorySpace.HBM)],
+        out_specs=[vmem, vmem],
         scratch_shapes=[pltpu.VMEM((nsrc + 2 * HALO, depth, nbins), jnp.bfloat16),
                         pltpu.SemaphoreType.DMA((nsrc + 2 * HALO,))],
-        compiler_params=pltpu.CompilerParams(vmem_limit_bytes=24 << 20),
+        compiler_params=pltpu.CompilerParams(vmem_limit_bytes=60 << 20),
         name="pick",
     )(sources, flags2.T, spec)
 
@@ -359,9 +368,9 @@
                         pltpu.SemaphoreType.DMA((6, half)), pltpu.SemaphoreType.DMA((6, half)),
                         pltpu.SemaphoreType.DMA((2,)), pltpu.SemaphoreType.DMA((2,))],
         compiler_params=pltpu.CompilerParams(
-            collective_id=0, has_side_effects=True, vmem_limit_bytes=40 << 20),
+            collective_id=0, has_side_effects=True, vmem_limit_bytes=24 << 20),
         name="share",
-    )(picked[:nsrc].reshape(nchunk, crow, nbins), picked[nsrc:])
+    )(picked.reshape(nchunk, crow, nbins), edges)
     src = src.reshape(nsrc, depth, nbins)
 
     fb = 128
@@ -379,11 +388,11 @@
                   pl.BlockSpec((2 * HALO, depth, fb), by_f),
                   pl.BlockSpec((nlags, nlags), lambda at: (0, 0))],
         out_specs=pl.BlockSpec((sgroup, nchan, nlags), lambda at: (jnp.maximum(at - steps, 0), 0, 0)),
-        scratch_shapes=[pltpu.VMEM((nrow * fb, depth), jnp.float32),
-                        pltpu.VMEM((2 * nsrc * fb, depth), jnp.float32),
-                        pltpu.VMEM((nbins * 2 * nsrc, 128), jnp.float32),
-                        pltpu.VMEM((sgroup * nrow, nlags), jnp.float32)],
-        compiler_params=pltpu.CompilerParams(vmem_limit_bytes=56 << 20),
+        scratch_shapes=[pltpu.VMEM((nrow * (fb + 1), depth), jnp.float32),
+                        pltpu.VMEM((2 * nsrc * (fb + 1), depth), jnp.float32),
+                        pltpu.VMEM((nbins * (2 * nsrc + 1), 128), jnp.float32),
+                        pltpu.VMEM((nlags // 128, sgroup * nrow, 128), jnp.float32)],
+        compiler_params=pltpu.CompilerParams(vmem_limit_bytes=38 << 20),
         name="lags",
     )(spec, flags2, src, halo, jnp.asarray(make_table(nbins, nlags)))
 

time: 116 us -> 97 us (0.84)
  Pallas kernels: 108 us -> 88.9 us
    pallas_call x1, Pallas kernels: 49.6 us -> 31.4 us  [local(): pl.pallas_call(functools.partial(lag_kernel, nwin, nrow, sgroup), grid=(s...]
where the time goes in v3:
time: 97 us; the launch traced here: 96.7 us
  Pallas kernels  88.9 us (92%)
  local copies, waits for them, and re-layouts  6.89 us (7%)
    pallas_call x1, Pallas kernels, local(): pl.pallas_call(functools.partial(share_kernel, outer, inner, nchunk), out...  52.2 us
    pallas_call x1, Pallas kernels, local(): pl.pallas_call(functools.partial(lag_kernel, nwin, nrow, sgroup), grid=(s...  31.4 us
    unnamed x8, local copies, waits for them, and re-layouts  6.16 us
    pallas_call x1, Pallas kernels, local(): pl.pallas_call(functools.partial(pick_kernel, nsrc), out_shape=[jax.Shape...  5.32 us

profile of v3, /device:TPU:0, one launch (start us, length us, event | category | flops | bytes accessed | tf_op | source)
XLA Modules:
  0.0 96.7 jit_solution(8022547791485434998)
XLA Ops:
  0.0 0.8 convert_element_type.3
  0.8 0.1 fusion
  0.8 0.7 copy.5.mask_ref
  1.6 5.3 %pick.1 = (bf16[16,128,512]{2,1,0:T(8,128)(2,1)}, bf16[4,128,512]{2,1,0:T(8,128)(2,1)}) custom-call(s32[16]{0:T(128)} %src_ref.1, f32[128,64]{1,0:T(8,128)} %copy.5.mask_ref, bf16[64,128,512]{2,1,0:T(8,128)(2,1)} %bitcast.5), custom_call_target="tpu_custom_call" | custom-call | tf_op jit(solution)/shard_map/pick/pallas_call | solution.py:340
  6.9 0.0 copy-start.1
  6.9 0.0 copy-start.2
  6.9 1.7 %copy-done.2 = bf16[16,128,512]{2,1,0:T(8,128)(2,1)S(1)} copy-done((bf16[16,128,512]{2,1,0:T(8,128)(2,1)S(1)}, bf16[16,128,512]{2,1,0:T(8,128)(2,1)}, u32[]{:S(2)}) %copy-start.2) | copy-done | bytes 2097176
  8.7 0.0 copy-start.3
  8.7 1.0 %copy-done.3 = bf16[4,128,512]{2,1,0:T(8,128)(2,1)S(1)} copy-done((bf16[4,128,512]{2,1,0:T(8,128)(2,1)S(1)}, bf16[4,128,512]{2,1,0:T(8,128)(2,1)}, u32[]{:S(2)}) %copy-start.3) | copy-done | bytes 524312
  9.7 52.2 %share.1 = (bf16[32,64,512]{2,1,0:T(8,128)(2,1)S(1)}, bf16[4,128,512]{2,1,0:T(8,128)(2,1)S(1)}) custom-call(bf16[32,64,512]{2,1,0:T(8,128)(2,1)S(1)} %bitcast.8, bf16[4,128,512]{2,1,0:T(8,128)(2,1)S(1)} %copy-done.3), custom_call_target="tpu_custom_call" | custom-call | tf_op jit(solution)/shard_map/share/pallas_call | solution.py:361
  61.9 0.0 copy-done.1
  61.9 0.0 copy-start
  62.0 3.4 %copy-done = bf16[64,2,64,512]{3,2,1,0:T(8,128)(2,1)S(1)} copy-done((bf16[64,2,64,512]{3,2,1,0:T(8,128)(2,1)S(1)}, bf16[64,2,64,512]{3,2,1,0:T(8,128)(2,1)}, u32[]{:S(2)}) %copy-start) | copy-done | bytes 8388632
  65.3 31.4 %lags.1 = f32[16,64,1024]{2,1,0:T(8,128)} custom-call(bf16[64,128,512]{2,1,0:T(8,128)(2,1)S(1)} %bitcast.6, f32[64,128]{1,0:T(8,128)S(1)} %get-tuple-element.14.valid_ref, bf16[16,128,512]{2,1,0:T(8,128)(2,1)S(1)} %bitcast.7, bf16[4,128,512]{2,1,0:T(8,128)(2,1)S(1)} %get-tuple-element.12.halo_ref, bf16[1024,1024]{1,0:T(8,128)(2,1)S(1)} %copy-done.1), custom_call_target="tpu_custom_call" | custom-call | tf_op jit(solution)/shard_map/lags/pallas_call | solution.py:381
Async XLA Ops:
  6.9 55.0 %copy-start.1 = (bf16[1024,1024]{1,0:T(8,128)(2,1)S(1)}, bf16[1024,1024]{1,0:T(8,128)(2,1)}, u32[]{:S(2)}) copy-start(bf16[1024,1024]{1,0:T(8,128)(2,1)} %constant.2.clone.table_ref) | copy-start | bytes 6291460
  6.9 1.7 %copy-start.2 = (bf16[16,128,512]{2,1,0:T(8,128)(2,1)S(1)}, bf16[16,128,512]{2,1,0:T(8,128)(2,1)}, u32[]{:S(2)}) copy-start(bf16[16,128,512]{2,1,0:T(8,128)(2,1)} %get-tuple-element.9) | copy-start | bytes 6291460
  8.7 1.0 %copy-start.3 = (bf16[4,128,512]{2,1,0:T(8,128)(2,1)S(1)}, bf16[4,128,512]{2,1,0:T(8,128)(2,1)}, u32[]{:S(2)}) copy-start(bf16[4,128,512]{2,1,0:T(8,128)(2,1)} %get-tuple-element.10.edge_ref) | copy-start | bytes 1572868
  61.9 3.4 %copy-start = (bf16[64,2,64,512]{3,2,1,0:T(8,128)(2,1)S(1)}, bf16[64,2,64,512]{3,2,1,0:T(8,128)(2,1)}, u32[]{:S(2)}) copy-start(bf16[64,2,64,512]{3,2,1,0:T(8,128)(2,1)} %param.4) | copy-start | bytes 25165828

commit v4 on v3

--- a/solution.py
+++ b/solution.py
@@ -10,7 +10,7 @@
 
 MESH = pl.DeviceIdType.MESH
 HALO = 2
-LAG = 2
+LAG = 4
 
 
 def make_table(nbins, nlags):
@@ -182,14 +182,6 @@
 
     lax.fori_loop(0, half, send_across, 0)
 
-    @pl.when(me < size - 1)
-    def _():
-        to_after().start()
-
-    @pl.when(me > 0)
-    def _():
-        to_before().start()
-
     @pl.when(me == 0)
     def _():
         halo_ref[0:HALO] = jnp.zeros((HALO,) + halo_ref.shape[1:], halo_ref.dtype)
@@ -216,6 +208,16 @@
         def leave(k):
             finish(1, second, k, out_ref, core * half + k)
             back(k).start()
+
+        @pl.when(t == half)
+        def _():
+            @pl.when(me < size - 1)
+            def _():
+                to_after().start()
+
+            @pl.when(me > 0)
+            def _():
+                to_before().start()
 
         guarded(t, True, enter)
         relay(0, first, t - ready)
@@ -345,7 +347,7 @@
         out_specs=[vmem, vmem],
         scratch_shapes=[pltpu.VMEM((nsrc + 2 * HALO, depth, nbins), jnp.bfloat16),
                         pltpu.SemaphoreType.DMA((nsrc + 2 * HALO,))],
-        compiler_params=pltpu.CompilerParams(vmem_limit_bytes=60 << 20),
+        compiler_params=pltpu.CompilerParams(vmem_limit_bytes=57 << 20),
         name="pick",
     )(sources, flags2.T, spec)
 
@@ -354,7 +356,7 @@
     while (2 * inner) ** 2 <= chips and chips % (2 * inner) == 0:
         inner *= 2
     outer = chips // inner
-    cut = 2
+    cut = 4
     nchunk, crow = nsrc * cut, depth // cut
     half = nchunk // 2
     chunk = lambda *lead: pltpu.VMEM(lead + (crow, nbins), jnp.bfloat16)
@@ -392,7 +394,7 @@
                         pltpu.VMEM((2 * nsrc * (fb + 1), depth), jnp.float32),
                         pltpu.VMEM((nbins * (2 * nsrc + 1), 128), jnp.float32),
                         pltpu.VMEM((nlags // 128, sgroup * nrow, 128), jnp.float32)],
-        compiler_params=pltpu.CompilerParams(vmem_limit_bytes=38 << 20),
+        compiler_params=pltpu.CompilerParams(vmem_limit_bytes=56 << 20),
         name="lags",
     )(spec, flags2, src, halo, jnp.asarray(make_table(nbins, nlags)))
 

time: 97 us -> 91.4 us (0.942)
  Pallas kernels: 88.9 us -> 84 us
  local copies, waits for them, and re-layouts: 6.89 us -> 5.5 us
    pallas_call x1, Pallas kernels: 52.2 us -> 46.5 us  [local(): pl.pallas_call(functools.partial(share_kernel, outer, inner, nchunk), out...]
    unnamed x8, local copies, waits for them, and re-layouts: 6.16 us -> 4.78 us
where the time goes in v4:
time: 91.4 us; the launch traced here: 91 us
  Pallas kernels  84 us (92%)
  local copies, waits for them, and re-layouts  5.5 us (6%)
  other arithmetic  1.46 us (2%)
    pallas_call x1, Pallas kernels, local(): pl.pallas_call(functools.partial(share_kernel, outer, inner, nchunk), out...  46.5 us
    pallas_call x1, Pallas kernels, local(): pl.pallas_call(functools.partial(lag_kernel, nwin, nrow, sgroup), grid=(s...  32.3 us
    pallas_call x1, Pallas kernels, local(): pl.pallas_call(functools.partial(pick_kernel, nsrc), out_shape=[jax.Shape...  5.26 us
    unnamed x8, local copies, waits for them, and re-layouts  4.78 us

profile of v4, /device:TPU:0, one launch (start us, length us, event | category | flops | bytes accessed | tf_op | source)
XLA Modules:
  0.0 91.0 jit_solution(10942857993209255445)
XLA Ops:
  0.0 0.8 convert_element_type.3
  0.8 0.7 fusion
  1.5 0.7 copy.5.mask_ref
  2.2 5.3 %pick.1 = (bf16[16,128,512]{2,1,0:T(8,128)(2,1)}, bf16[4,128,512]{2,1,0:T(8,128)(2,1)}) custom-call(s32[16]{0:T(128)} %src_ref.1, f32[128,64]{1,0:T(8,128)} %copy.5.mask_ref, bf16[64,128,512]{2,1,0:T(8,128)(2,1)} %bitcast.7), custom_call_target="tpu_custom_call" | custom-call | tf_op jit(solution)/shard_map/pick/pallas_call | solution.py:342
  7.4 0.0 copy-start.1
  7.5 1.6 %copy-done.1 = bf16[16,128,512]{2,1,0:T(8,128)(2,1)S(1)} copy-done((bf16[16,128,512]{2,1,0:T(8,128)(2,1)S(1)}, bf16[16,128,512]{2,1,0:T(8,128)(2,1)}, u32[]{:S(2)}) %copy-start.1) | copy-done | bytes 2097176
  9.0 0.0 copy-start.3
  9.0 1.0 %copy-done.3 = bf16[4,128,512]{2,1,0:T(8,128)(2,1)S(1)} copy-done((bf16[4,128,512]{2,1,0:T(8,128)(2,1)S(1)}, bf16[4,128,512]{2,1,0:T(8,128)(2,1)}, u32[]{:S(2)}) %copy-start.3) | copy-done | bytes 524312
  10.1 46.5 %share.1 = (bf16[64,32,512]{2,1,0:T(8,128)(2,1)S(1)}, bf16[4,128,512]{2,1,0:T(8,128)(2,1)S(1)}) custom-call(bf16[64,32,512]{2,1,0:T(8,128)(2,1)S(1)} %bitcast.6, bf16[4,128,512]{2,1,0:T(8,128)(2,1)S(1)} %copy-done.3), custom_call_target="tpu_custom_call" | custom-call | tf_op jit(solution)/shard_map/share/pallas_call | solution.py:363
  56.6 0.0 copy-start
  56.6 1.3 %copy-done = bf16[64,32,512]{2,1,0:T(8,128)(2,1)} copy-done((bf16[64,32,512]{2,1,0:T(8,128)(2,1)}, bf16[64,32,512]{2,1,0:T(8,128)(2,1)S(1)}, u32[]{:S(2)}) %copy-start) | copy-done | bytes 2097176
  58.0 0.0 copy-start.2
  58.0 0.8 copy-done.2
  58.8 32.3 %lags.1 = f32[16,64,1024]{2,1,0:T(8,128)} custom-call(bf16[64,128,512]{2,1,0:T(8,128)(2,1)} %bitcast.8, f32[64,128]{1,0:T(8,128)} %get-tuple-element.14.valid_ref, bf16[16,128,512]{2,1,0:T(8,128)(2,1)} %bitcast.5, bf16[4,128,512]{2,1,0:T(8,128)(2,1)} %copy-done.2, bf16[1024,1024]{1,0:T(8,128)(2,1)} %constant.2.clone.table_ref), custom_call_target="tpu_custom_call" | custom-call | tf_op jit(solution)/shard_map/lags/pallas_call | solution.py:383
Async XLA Ops:
  7.4 1.6 %copy-start.1 = (bf16[16,128,512]{2,1,0:T(8,128)(2,1)S(1)}, bf16[16,128,512]{2,1,0:T(8,128)(2,1)}, u32[]{:S(2)}) copy-start(bf16[16,128,512]{2,1,0:T(8,128)(2,1)} %get-tuple-element.9) | copy-start | bytes 6291460
  9.0 1.0 %copy-start.3 = (bf16[4,128,512]{2,1,0:T(8,128)(2,1)S(1)}, bf16[4,128,512]{2,1,0:T(8,128)(2,1)}, u32[]{:S(2)}) copy-start(bf16[4,128,512]{2,1,0:T(8,128)(2,1)} %get-tuple-element.10.edge_ref) | copy-start | bytes 1572868
  56.6 1.4 %copy-start = (bf16[64,32,512]{2,1,0:T(8,128)(2,1)}, bf16[64,32,512]{2,1,0:T(8,128)(2,1)S(1)}, u32[]{:S(2)}) copy-start(bf16[64,32,512]{2,1,0:T(8,128)(2,1)S(1)} %get-tuple-element.11) | copy-start | bytes 6291460
  58.0 0.8 copy-start.2
